TPU v7x, 32 devices: a whole 2x2x4 slice. The times are simulated.
32 devices in a mesh: groups: 2 (over x), gx: 16 (over z, y, core).
Axes of the slice: x: 2, y: 2, z: 4, core: 2. Of those that a mesh axis runs over, the one named last changes fastest.
Arguments:
- snapshots: bfloat16 [256, 4, 512, 128], P('gx', None, 'groups'), parts along dimension 2, may hold values from -20 to 20
- cell_weights: float32 [512, 128], P(('groups', 'gx')), parts along dimension 0, may hold values from 0.5 to 4.5
- diffusivity: float32 [4, 512, 128], P(None, ('groups', 'gx')), parts along dimension 1, may hold values from 0.2 to 2
Outputs:
- diffused_modes: bfloat16 [256, 4, 512, 128], P(None, None, ('groups', 'gx')), parts along dimension 2
- reduced_operator: float32 [512, 256], P('groups'), parts along dimension 0
There are 2 independent parts, one for each index of `groups`. A program takes and returns all parts, laid end to end along the dimension named above; each array names one. Nothing has to cross between parts.
All inputs are finite; a program needn't handle non-finite values.
Results may differ from a plain program's by a relative error of at most 0.0005.
Values may be sent and summed in bfloat16 or wider, within the bound.
A program may use at most 128 MiB of HBM per device.

v0:
```python
import jax
import jax.numpy as jnp
from jax import lax
from jax.sharding import PartitionSpec as P


def extended(block, sides, width):
    for axis, dim in sides:
        count = lax.axis_size(axis)
        forward = [(i, i + 1) for i in range(count - 1)]
        backward = [(target, source) for source, target in forward]
        low = lax.ppermute(
            lax.slice_in_dim(block, block.shape[dim] - width, None, axis=dim), axis, forward
        )
        high = lax.ppermute(lax.slice_in_dim(block, 0, width, axis=dim), axis, backward)
        block = jnp.concatenate([low, block, high], axis=dim)
    return block


def stencil_apply(padded_x, diffusivity):
    field = padded_x[:, :, 2:-2]
    along_x = (
        -padded_x[:, :, :-4]
        + 16.0 * padded_x[:, :, 1:-3]
        - 30.0 * field
        + 16.0 * padded_x[:, :, 3:-1]
        - padded_x[:, :, 4:]
    ) / 12.0
    padded_y = jnp.pad(field, ((0, 0), (0, 0), (0, 0), (2, 2)))
    along_y = (
        -padded_y[..., :-4]
        + 16.0 * padded_y[..., 1:-3]
        - 30.0 * field
        + 16.0 * padded_y[..., 3:-1]
        - padded_y[..., 4:]
    ) / 12.0
    return diffusivity * (along_x + along_y)


def make_rotation(gram_total):
    lower_factor = jnp.linalg.cholesky(gram_total)
    identity = jnp.eye(gram_total.shape[0], dtype=jnp.float32)
    return jax.scipy.linalg.solve_triangular(lower_factor, identity, lower=True)


def on_device(snapshots, cell_weights, diffusivity):
    highest = lax.Precision.HIGHEST
    pod_block = lax.all_to_all(snapshots, "gx", split_axis=2, concat_axis=0, tiled=True)
    snap_float = pod_block.astype(jnp.float32)
    gram_part = jnp.einsum(
        "svxy,tvxy->st", snap_float, snap_float * cell_weights, precision=highest
    )
    cell_count = pod_block.shape[1] * pod_block.shape[2] * pod_block.shape[3] * lax.axis_size("gx")
    padded_raw = extended(pod_block, (("gx", 2),), 2)
    diffused_raw = stencil_apply(padded_raw.astype(jnp.float32), diffusivity)
    cross_part = jnp.einsum(
        "svxy,tvxy->st", snap_float * cell_weights, diffused_raw, precision=highest
    )
    gram_sum_all, cross_sum_all = lax.psum((gram_part, cross_part), "gx")
    rotation = make_rotation(gram_sum_all / cell_count)
    cross_total = cross_sum_all / cell_count
    reduced = jnp.dot(
        jnp.dot(rotation, cross_total, precision=highest), rotation.T, precision=highest
    )
    diffused = jnp.einsum("st,tvxy->svxy", rotation, diffused_raw, precision=highest)
    return (diffused.astype(jnp.bfloat16), reduced)


def solution(mesh):
    in_specs = (
        P("gx", None, "groups", None),
        P(("groups", "gx"), None),
        P(None, ("groups", "gx"), None),
    )
    out_specs = (P(None, None, ("groups", "gx"), None), P("groups", None))
    return jax.shard_map(
        on_device, mesh=mesh, in_specs=in_specs, out_specs=out_specs, check_vma=False
    )
```

profile of v0, /device:TPU:0, one launch (start us, length us, event | category | flops | bytes accessed | tf_op | source)
XLA Modules:
  0.0 353.1 jit_solution(6415887800945460660)
XLA Ops:
  7.2 0.0 copy-start.3
  7.2 6.9 %copy.12 = bf16[16,4,256,128]{3,0,1,2:T(8,128)(2,1)} copy(bf16[16,4,256,128]{3,2,1,0:T(8,128)(2,1)} %param.3) | data formatting | bytes 8388608 | tf_op args[0]
  14.1 7.6 %all-to-all-start = ((bf16[16,4,256,128]{3,0,1,2:T(8,128)(2,1)}), bf16[16,4,256,128]{3,0,1,2:T(8,128)(2,1)}, u32[]{:S(2)}, u32[]{:S(2)}) async-start(bf16[16,4,256,128]{3,0,1,2:T(8,128)(2,1)} %copy.12), calls=%async_computation | async-start | bytes 8388608 | tf_op jit(solution)/shard_map/all_to_all | solution.py:48
  21.7 0.0 all-reduce.5.cloned.1.call-start
  21.7 0.0 copy-done.3
  21.8 77.5 %all-to-all-done = bf16[16,4,256,128]{3,0,1,2:T(8,128)(2,1)} async-done(((bf16[16,4,256,128]{3,0,1,2:T(8,128)(2,1)}), bf16[16,4,256,128]{3,0,1,2:T(8,128)(2,1)}, u32[]{:S(2)}, u32[]{:S(2)}) %all-to-all-start) | async-done | bytes 4194336 | tf_op jit(solution)/shard_map/all_to_all | solution.py:48
  99.2 3.4 copy.13
  102.6 0.0 copy-start
  102.6 0.1 fusion.37
  102.7 2.9 collective-permute-start
  105.7 1.5 collective-permute-start.1
  107.1 0.0 copy-done.2
  107.1 3.3 convert_multiply_fusion
  110.4 4.5 %convolution_bitcast_fusion = f32[256,256]{0,1:T(8,128)} fusion(f32[256,4,16,128]{3,0,2,1:T(8,128)S(1)} %bitcast.59, bf16[256,4,16,128]{3,0,2,1:T(8,128)(2,1)S(1)} %bitcast.56), kind=kOutput, calls=%fused_computation.30 | convolution fusion | flops 6442450944 | bytes 12845056 | tf_op jit(solution)/shard_map/svxy,tvxy->st/dot_general | solution.py:50
  114.9 0.0 copy-done
  114.9 0.0 collective-permute-done
  114.9 0.0 collective-permute-done.1
  114.9 2.7 maximum_convert_fusion
  117.6 3.8 %slice.107 = f32[256,4,16,128]{3,0,2,1:T(8,128)} slice(f32[256,4,20,128]{3,0,2,1:T(8,128)S(1)} %maximum_convert_fusion), slice={[0:256], [0:4], [2:18], [0:128]} | slice | bytes 16777216 | tf_op jit(solution)/shard_map/slice | solution.py:21
  121.4 24.1 %fusion.6 = f32[256,4,16,128]{3,0,2,1:T(8,128)} fusion(f32[256,4,16,128]{3,0,2,1:T(8,128)} %slice.107, f32[256,4,20,128]{3,0,2,1:T(8,128)S(1)} %maximum_convert_fusion, f32[4,16,128]{2,1,0:T(8,128)S(1)} %broadcast_multiply_fusion.1), kind=kLoop, calls=%fused_computation.12 | loop fusion | flops 35651584 | bytes 50364416 | tf_op jit(solution)/shard_map/mul | solution.py:37
  145.5 11.3 %fusion.16 = f32[256,256]{0,1:T(8,128)} fusion(f32[256,4,16,128]{3,0,2,1:T(8,128)} %fusion.6, bf16[256,4,16,128]{3,0,2,1:T(8,128)(2,1)} %bitcast.58, f32[16,128]{1,0:T(8,128)S(1)} %copy-done.2), kind=kOutput, calls=%fused_computation.29 | convolution fusion | flops 6446645248 | bytes 12853248 | tf_op jit(solution)/shard_map/svxy,tvxy->st/dot_general | solution.py:56
  156.7 0.0 all-reduce.5.cloned.1.call-update
  156.8 109.7 %all-reduce.5.cloned.1.call-done = (f32[256,256]{0,1:T(8,128)}, f32[256,256]{0,1:T(8,128)}) async-done(((f32[256,256]{0,1:T(8,128)}, f32[256,256]{0,1:T(8,128)}), (f32[256,256]{0,1:T(8,128)}, f32[256,256]{0,1:T(8,128)})) %all-reduce.5.cloned.1.call-update) | async-done | bytes 524304 | tf_op jit(solution)/shard_map/psum | solution.py:59
  266.5 1.0 broadcast_multiply_fusion
  267.5 0.1 copy.14
  267.6 1.0 fusion.20
  268.6 11.7 %cholesky.50 = f32[128,128]{1,0:T(8,128)S(1)} custom-call(f32[128,128]{1,0:T(8,128)S(1)} %cholesky.118), custom_call_target="Cholesky" | custom-call | tf_op jit(solution)/shard_map/jit(cholesky)/cholesky | solution.py:41
  280.4 9.8 %custom-call.15 = f32[1,128,128]{1,2,0:T(8,128)S(1)} custom-call(f32[1,128,128]{2,1,0:T(8,128)S(1)} %get-tuple-element.33), custom_call_target="InvertDiagBlocksLowerTriangular" | custom-call | tf_op jit(solution)/shard_map/jit(cholesky)/cholesky | solution.py:41
  290.2 0.2 constant_dynamic-update-slice_fusion.1
  290.5 0.3 convolution_subtract_fusion.1
  290.7 11.7 %cholesky.105 = f32[128,128]{1,0:T(8,128)S(1)} custom-call(f32[128,128]{1,0:T(8,128)S(1)} %convolution_subtract_fusion.1), custom_call_target="Cholesky" | custom-call | tf_op jit(solution)/shard_map/jit(cholesky)/cholesky | solution.py:41
  302.5 0.7 compare_reduce_fusion
  304.6 0.1 triangular_solve.63
  304.6 4.1 %while.1 = (s32[]{:T(128)}, f32[256,256]{1,0:T(8,128)S(1)}, s32[2,2]{1,0:T(2,128)S(1)}, f32[2,128,128]{2,1,0:T(8,128)S(1)}, s32[]{:T(128)}) while((s32[]{:T(128)}, f32[256,256]{1,0:T(8,128)S(1)}, s32[2,2]{1,0:T(2,128)S(1)}, f32[2,128,128]{2,1,0:T(8,128)S(1)}, s32[]{:T(128)}) %tuple.31), condition=%wide.while_cond, body=%wide.while_body.sunk | while | flops 2 | bytes 131189 | solution.py:43
  304.6 0.6 fusion.48
  305.2 1.4 bitcast_dynamic-update-slice_fusion.2
  306.7 0.6 fusion.48
  307.2 1.4 bitcast_dynamic-update-slice_fusion.2
  308.7 19.9 %custom-call.16 = f32[2,128,128]{1,2,0:T(8,128)S(1)} custom-call(f32[2,128,128]{2,1,0:T(8,128)S(1)} %get-tuple-element.9), custom_call_target="InvertDiagBlocksLowerTriangular" | custom-call | tf_op jit(solution)/shard_map/jit(_solve_triangular)/triangular_solve | solution.py:43
  328.6 0.3 fusion.25
  328.9 0.3 convolution_subtract_fusion
  329.2 0.3 fusion.28
  329.5 0.0 copy-start.1
  329.5 10.0 %convolution_convert_fusion = bf16[256,4,16,128]{3,0,2,1:T(8,128)(2,1)S(1)} fusion(f32[256,4,16,128]{3,0,2,1:T(8,128)} %fusion.6, f32[128,256]{1,0:T(8,128)S(1)} %fusion.28, f32[128,256]{1,0:T(8,128)S(1)} %fusion.25), kind=kOutput, calls=%fused_computation.28 | convolution fusion | flops 6444613632 | bytes 12845056 | tf_op jit(solution)/shard_map/st,tvxy->svxy/dot_general | solution.py:65
  339.5 4.7 %copy.16 = bf16[256,4,16,128]{3,2,1,0:T(8,128)(2,1)} copy(bf16[256,4,16,128]{3,0,2,1:T(8,128)(2,1)S(1)} %convolution_convert_fusion) | data formatting | bytes 8388608
  344.2 0.0 copy-done.1
  344.2 0.4 fusion.21
  344.7 1.1 fusion.23
  (12 shorter events, 0.2 us)
Async XLA Ops:
  7.2 14.6 %copy-start.3 = (f32[4,16,128]{2,1,0:T(8,128)S(1)}, f32[4,16,128]{2,1,0:T(8,128)}, u32[]{:S(2)}) copy-start(f32[4,16,128]{2,1,0:T(8,128)} %param.5) | copy-start | bytes 98308
  14.1 93.1 %copy-start.2 = (f32[16,128]{1,0:T(8,128)S(1)}, f32[16,128]{1,0:T(8,128)}, u32[]{:S(2)}) copy-start(f32[16,128]{1,0:T(8,128)} %param.4) | copy-start | bytes 24580
  14.1 85.1 %all-to-all-start = ((bf16[16,4,256,128]{3,0,1,2:T(8,128)(2,1)}), bf16[16,4,256,128]{3,0,1,2:T(8,128)(2,1)}, u32[]{:S(2)}, u32[]{:S(2)}) async-start(bf16[16,4,256,128]{3,0,1,2:T(8,128)(2,1)} %copy.12), calls=%async_computation | async-start | bytes 8388608 | tf_op jit(solution)/shard_map/all_to_all | solution.py:48
  21.7 244.8 %all-reduce.5.cloned.1.call-start = ((), (), s32[]{:S(2)}) async-start(), calls=%async_computation.1 | async-start | bytes 1048576 | tf_op jit(solution)/shard_map/psum | solution.py:59
  102.6 12.3 %copy-start = (bf16[16,4,16,16,128]{4,0,2,3,1:T(8,128)(2,1)}, bf16[16,4,16,16,128]{4,0,2,3,1:T(8,128)(2,1)S(1)}, u32[]{:S(2)}) copy-start(bf16[16,4,16,16,128]{4,0,2,3,1:T(8,128)(2,1)S(1)} %copy.13) | copy-start | bytes 12582916
  102.7 12.2 %collective-permute-start = (bf16[256,4,2,128]{3,0,2,1:T(8,128)(2,1)S(1)}, bf16[256,4,2,128]{3,0,2,1:T(8,128)(2,1)S(1)}, u32[]{:S(2)}, u32[]{:S(2)}) collective-permute-start(bf16[256,4,2,128]{3,0,2,1:T(8,128)(2,1)S(1)} %get-tuple-element.28), channel_id=1, source_target_pairs={{0,1},{1,2},{2,3},{3,4},{4,5},{5,6},{6,7},{7,8},{8,9},{9,10},{10,1... | collective-permute-start | bytes 1572872 | tf_op jit(solution)/shard_map/ppermute | solution.py:12
  105.7 9.3 %collective-permute-start.1 = (bf16[256,4,2,128]{3,0,2,1:T(8,128)(2,1)S(1)}, bf16[256,4,2,128]{3,0,2,1:T(8,128)(2,1)S(1)}, u32[]{:S(2)}, u32[]{:S(2)}) collective-permute-start(bf16[256,4,2,128]{3,0,2,1:T(8,128)(2,1)S(1)} %get-tuple-element.29), channel_id=1, source_target_pairs={{1,0},{2,1},{3,2},{4,3},{5,4},{6,5},{7,6},{8,7},{9,8},{10,9},{11,1... | collective-permute-start | bytes 1572872 | tf_op jit(solution)/shard_map/ppermute | solution.py:15
  329.5 14.8 %copy-start.1 = (f32[256,256]{0,1:T(8,128)S(1)}, f32[256,256]{0,1:T(8,128)}, u32[]{:S(2)}) copy-start(f32[256,256]{0,1:T(8,128)} %get-tuple-element.25) | copy-start | bytes 786436
Sparse Core Ops, SparseCore 0:
  156.9 109.5 all-reduce.4
where the time goes:
time: 357 us; the launch traced here: 353 us
  waiting for transfers between devices  187 us (52%)
  other arithmetic  86 us (24%)
  matrix products  28.6 us (8%)
  local copies, waits for them, and re-layouts  23.1 us (6%)
  between operations  16 us (4%)
  starting transfers between devices  12 us (3%)
    psum x1, waiting for transfers between devices, on_device(): gram_sum_all, cross_sum_all = lax.psum((gram_part, cross_part), 'gx')  110 us
    all_to_all x1, waiting for transfers between devices, on_device(): lax.all_to_all(snapshots, 'gx', split_axis=2, concat_axis=0, tiled=True)  77.5 us
    another operation x6, other arithmetic, make_rotation(): lower_factor = jnp.linalg.cholesky(gram_total)  34 us
    mul x2, other arithmetic, stencil_apply(): return diffusivity * (along_x + along_y)  24.1 us
    another operation x3, other arithmetic, make_rotation(): return jax.scipy.linalg.solve_triangular(lower_factor, identity, lower=True)  20 us
    unnamed x10, local copies, waits for them, and re-layouts  11.6 us
    dot_general x1, matrix products, on_device(): jnp.einsum('svxy,tvxy->st', snap_float * cell_weights, diffused_raw, prec...  11.3 us
    dot_general x1, matrix products, on_device(): jnp.einsum('st,tvxy->svxy', rotation, diffused_raw, precision=highest)  10 us
  transfers between devices with their start and end apart: 4, of which 2 were waited for; matrix products, arithmetic and copies ran while one was open for 2% of the time, Pallas kernels for 0%

commit v1 on v0

v1 whole, which is shorter than its diff:
```python
import functools

import jax
import jax.numpy as jnp
from jax import lax
from jax.experimental import pallas as pl
from jax.experimental.pallas import tpu as pltpu
from jax.sharding import PartitionSpec as P

MESH = pl.DeviceIdType.MESH
HIGHEST = lax.Precision.HIGHEST
NT = (((1,), (1,)), ((), ()))
TN = (((0,), (0,)), ((), ()))
PACK = 16
PIVOTS = 32


def iota(shape, dim):
    return lax.broadcasted_iota(jnp.int32, shape, dim)


def swap_matrix(outer, inner):
    size = outer * inner
    row, col = iota((size, size), 0), iota((size, size), 1)
    source = lax.rem(row, inner) * outer + lax.div(row, inner)
    return jnp.where(col == source, 1.0, 0.0).astype(jnp.bfloat16)


def parts_of(value, count):
    parts = []
    for _ in range(count):
        part = value.astype(jnp.bfloat16)
        parts.append(part)
        value = value - part.astype(jnp.float32)
    return parts


def dot32(a, b, dims):
    return lax.dot_general(a, b, dims, preferred_element_type=jnp.float32)


def gather_kernel(n, snap_ref, weight_ref, diff_ref, x_ref, gram_ref, cross_ref,
                  pod, local_sem, send_sem, recv_sem, halo_send, halo_recv):
    me = lax.axis_index("gx")
    own, variables, _, cols = snap_ref.shape
    total, rows = pod.shape[0], pod.shape[2]

    barrier = pltpu.get_barrier_semaphore()

    def greet(k, carry):
        pl.semaphore_signal(
            barrier, inc=1, device_id={"gx": lax.rem(me + k, n)}, device_id_type=MESH
        )
        return carry

    lax.fori_loop(1, n, greet, 0)

    def own_copy(v):
        return pltpu.make_async_copy(
            snap_ref.at[:, v, pl.ds(me * rows, rows)],
            pod.at[pl.ds(me * own, own), v],
            local_sem.at[v],
        )

    for v in range(variables):
        own_copy(v).start()
    pl.semaphore_wait(barrier, n - 1)

    for v in range(variables):

        def send(k, carry, v=v):
            offset = lax.div(k, 2) + lax.rem(k, 2) * (n // 2)
            target = lax.rem(me + offset, n)
            pltpu.make_async_remote_copy(
                src_ref=snap_ref.at[:, v, pl.ds(target * rows, rows)],
                dst_ref=pod.at[pl.ds(me * own, own), v],
                send_sem=send_sem.at[v],
                recv_sem=recv_sem.at[v],
                device_id={"gx": target},
                device_id_type=MESH,
            ).start()
            return carry

        lax.fori_loop(1, n, send, 0)

    gram_ref[...] = jnp.zeros_like(gram_ref)
    cross_ref[...] = jnp.zeros_like(cross_ref)
    lane_gap = iota((cols, cols), 0) - iota((cols, cols), 1)
    band = jnp.where(lane_gap == 0, -60.0, 0.0)
    band = jnp.where(jnp.abs(lane_gap) == 1, 16.0, band)
    band = jnp.where(jnp.abs(lane_gap) == 2, -1.0, band).astype(jnp.bfloat16)
    swap = swap_matrix(rows, PACK)

    def all_but_own(v, sem):
        piece = pod.at[pl.ds(0, total - own), v]
        return pltpu.make_async_copy(piece, piece, sem.at[v])

    def to_low(v):
        return pltpu.make_async_remote_copy(
            src_ref=x_ref.at[v, pl.ds(2, 2)],
            dst_ref=x_ref.at[v, pl.ds(rows + 2, 2)],
            send_sem=halo_send.at[0, v],
            recv_sem=halo_recv.at[0, v],
            device_id={"gx": jnp.maximum(me - 1, 0)},
            device_id_type=MESH,
        )

    def to_high(v):
        return pltpu.make_async_remote_copy(
            src_ref=x_ref.at[v, pl.ds(rows, 2)],
            dst_ref=x_ref.at[v, pl.ds(0, 2)],
            send_sem=halo_send.at[1, v],
            recv_sem=halo_recv.at[1, v],
            device_id={"gx": jnp.minimum(me + 1, n - 1)},
            device_id_type=MESH,
        )

    for v in range(variables):
        own_copy(v).wait()
        all_but_own(v, recv_sem).wait()

        @pl.loop(0, total // PACK)
        def _(g):
            first = pl.multiple_of(g * PACK, PACK)
            block = pod[pl.ds(first, PACK), v].reshape(PACK * rows, cols)
            turned = dot32(swap, block, (((1,), (0,)), ((), ())))
            x_ref[v, pl.ds(2, rows), pl.ds(first, PACK), :] = turned.astype(
                jnp.bfloat16
            ).reshape(rows, PACK, cols)

        @pl.when(me > 0)
        def _():
            to_low(v).start()

        @pl.when(me < n - 1)
        def _():
            to_high(v).start()

        @pl.when(me == 0)
        def _():
            x_ref[v, 0:2] = jnp.zeros((2, total, cols), jnp.bfloat16)

        @pl.when(me == n - 1)
        def _():
            x_ref[v, rows + 2 : rows + 4] = jnp.zeros((2, total, cols), jnp.bfloat16)

        @pl.loop(0, rows // 2)
        def _(pair):
            at = 2 * pair
            plain, weighed = [], []
            for step in range(2):
                field = x_ref[v, at + step + 2]
                plain.append(field)
                weighed.append(field.astype(jnp.float32) * weight_ref[pl.ds(at + step, 1), :])
            left = jnp.concatenate(plain, axis=1)
            acc = gram_ref[...]
            for part in parts_of(jnp.concatenate(weighed, axis=1), 3):
                acc += dot32(left, part, NT)
            gram_ref[...] = acc

        @pl.when(me < n - 1)
        def _():
            to_low(v).wait_recv()
            to_high(v).wait_send()

        @pl.when(me > 0)
        def _():
            to_high(v).wait_recv()
            to_low(v).wait_send()

        @pl.loop(0, rows // 2)
        def _(pair):
            at = 2 * pair
            plain, weighed = [], []
            for step in range(2):
                near = [x_ref[v, at + step + k] for k in range(5)]
                wide = [near[k].astype(jnp.float32) for k in (0, 1, 3, 4)]
                spread = dot32(near[2], band, (((1,), (0,)), ((), ())))
                spread += 16.0 * (wide[1] + wide[2]) - (wide[0] + wide[3])
                scale = weight_ref[pl.ds(at + step, 1), :] * diff_ref[v, pl.ds(at + step, 1), :]
                plain.append(near[2])
                weighed.append(spread * (scale / 12.0))
            left = jnp.concatenate(plain, axis=1)
            acc = cross_ref[...]
            for part in parts_of(jnp.concatenate(weighed, axis=1), 3):
                acc += dot32(left, part, NT)
            cross_ref[...] = acc

    for v in range(variables):
        all_but_own(v, send_sem).wait()


def gather(n, snapshots, cell_weights, diffusivity):
    own, variables, _, cols = snapshots.shape
    rows = cell_weights.shape[0]
    total = own * n
    vmem = pl.BlockSpec(memory_space=pltpu.VMEM)
    square = jax.ShapeDtypeStruct((total, total), jnp.float32)
    return pl.pallas_call(
        functools.partial(gather_kernel, n),
        out_shape=(
            jax.ShapeDtypeStruct((variables, rows + 4, total, cols), jnp.bfloat16),
            square,
            square,
        ),
        in_specs=[pl.BlockSpec(memory_space=pl.ANY), vmem, vmem],
        out_specs=(vmem, vmem, vmem),
        scratch_shapes=[
            pltpu.VMEM((total, variables, rows, cols), jnp.bfloat16),
            pltpu.SemaphoreType.DMA((variables,)),
            pltpu.SemaphoreType.DMA((variables,)),
            pltpu.SemaphoreType.DMA((variables,)),
            pltpu.SemaphoreType.DMA((2, variables)),
            pltpu.SemaphoreType.DMA((2, variables)),
        ],
        compiler_params=pltpu.CompilerParams(collective_id=0, has_side_effects=True),
        name="gather",
    )(snapshots, cell_weights, diffusivity)


def factor_kernel(cells, gram_ref, cross_ref, rotation_ref, reduced_ref, work):
    size = gram_ref.shape[0]
    lanes = 128
    work[:, :size] = gram_ref[...] * (1.0 / cells)
    work[:, size:] = jnp.where(iota((size, size), 0) == iota((size, size), 1), 1.0, 0.0)
    row = iota((PIVOTS, lanes), 0)
    lane = iota((PIVOTS, lanes), 1)
    for first in range(0, size, PIVOTS):
        group, shift = first // lanes * lanes, first % lanes
        block = work[first : first + PIVOTS, group : group + lanes]
        if shift:
            block = pltpu.roll(block, lanes - shift, 1)
        block = jnp.where(lane < PIVOTS, block, jnp.where(lane == row + PIVOTS, 1.0, 0.0))
        for k in range(PIVOTS):
            pivot_row = block[k : k + 1, :]
            scaled = pivot_row * (1.0 / pivot_row[:, k : k + 1])
            column = jnp.where(row > k, block[:, k : k + 1], 0.0)
            block = block - column * scaled
        pivots = jnp.sum(jnp.where(lane == row, block, 0.0), axis=1, keepdims=True)
        inverse = pltpu.roll(block, lanes - PIVOTS, 1) / jnp.sqrt(pivots)
        stripe = jnp.dot(
            inverse[:, :PIVOTS],
            work[first : first + PIVOTS, :],
            precision=HIGHEST,
            preferred_element_type=jnp.float32,
        )
        rotation_ref[first : first + PIVOTS, :] = stripe[:, size:]
        if first + PIVOTS < size:
            work[...] -= lax.dot_general(
                stripe[:, :size],
                stripe,
                TN,
                precision=HIGHEST,
                preferred_element_type=jnp.float32,
            )
    rotation = rotation_ref[...]
    half = jnp.dot(
        rotation, cross_ref[...] * (1.0 / cells), precision=HIGHEST,
        preferred_element_type=jnp.float32,
    )
    reduced_ref[...] = lax.dot_general(
        half, rotation, NT, precision=HIGHEST, preferred_element_type=jnp.float32
    )


def factor(cells, gram, cross):
    size = gram.shape[0]
    vmem = pl.BlockSpec(memory_space=pltpu.VMEM)
    square = jax.ShapeDtypeStruct((size, size), jnp.float32)
    return pl.pallas_call(
        functools.partial(factor_kernel, float(cells)),
        out_shape=(square, square),
        in_specs=[vmem, vmem],
        out_specs=(vmem, vmem),
        scratch_shapes=[pltpu.VMEM((size, 2 * size), jnp.float32)],
        name="factor",
    )(gram, cross)


def modes_kernel(rotation_ref, diff_ref, x_ref, out_ref, field, turned):
    rows, cols = diff_ref.shape[1:]
    total = rotation_ref.shape[0]
    parts = parts_of(rotation_ref[...], 3)
    lane = iota((1, cols), 1)
    masks = {
        shift: jnp.where(
            (lane >= shift) & (lane < cols + shift), -1.0 if abs(shift) == 2 else 16.0, 0.0
        )
        for shift in (-2, -1, 1, 2)
    }

    @pl.loop(0, (rows + 4) // 2)
    def _(pair):
        right = jnp.concatenate([x_ref[0, 2 * pair], x_ref[0, 2 * pair + 1]], axis=1)
        acc = dot32(parts[0], right, (((1,), (0,)), ((), ())))
        for part in parts[1:]:
            acc += dot32(part, right, (((1,), (0,)), ((), ())))
        field[2 * pair] = acc[:, :cols]
        field[2 * pair + 1] = acc[:, cols:]

    @pl.loop(0, rows)
    def _(at):
        near = [field[at + k] for k in range(5)]
        spread = 16.0 * (near[1] + near[3]) - (near[0] + near[4]) - 60.0 * near[2]
        for shift in (-2, -1, 1, 2):
            spread += pltpu.roll(near[2], shift % cols, 1) * masks[shift]
        spread = spread * (diff_ref[0, pl.ds(at, 1), :] / 12.0)
        turned[at] = spread.astype(jnp.bfloat16)

    swap = swap_matrix(PACK, rows)

    @pl.loop(0, total // PACK)
    def _(g):
        first = pl.multiple_of(g * PACK, PACK)
        block = turned[:, pl.ds(first, PACK), :].reshape(rows * PACK, cols)
        out_ref[pl.ds(first, PACK), 0] = (
            dot32(swap, block, (((1,), (0,)), ((), ())))
            .astype(jnp.bfloat16)
            .reshape(PACK, rows, cols)
        )


def modes(rotation, diffusivity, fields):
    variables, rows, cols = diffusivity.shape
    total = rotation.shape[0]
    return pl.pallas_call(
        modes_kernel,
        out_shape=jax.ShapeDtypeStruct((total, variables, rows, cols), jnp.bfloat16),
        grid=(variables,),
        in_specs=[
            pl.BlockSpec((total, total), lambda v: (0, 0)),
            pl.BlockSpec((1, rows, cols), lambda v: (v, 0, 0)),
            pl.BlockSpec((1, rows + 4, total, cols), lambda v: (v, 0, 0, 0)),
        ],
        out_specs=pl.BlockSpec((total, 1, rows, cols), lambda v: (0, v, 0, 0)),
        scratch_shapes=[
            pltpu.VMEM((rows + 4, total, cols), jnp.float32),
            pltpu.VMEM((rows, total, cols), jnp.bfloat16),
        ],
        name="modes",
    )(rotation, diffusivity, fields)


def on_device(n, snapshots, cell_weights, diffusivity):
    variables, rows, cols = diffusivity.shape
    fields, gram, cross = gather(n, snapshots, cell_weights, diffusivity)
    gram, cross = lax.psum((gram, cross), "gx")
    rotation, reduced = factor(variables * rows * cols * n, gram, cross)
    return modes(rotation, diffusivity, fields), reduced


def solution(mesh):
    in_specs = (
        P("gx", None, "groups", None),
        P(("groups", "gx"), None),
        P(None, ("groups", "gx"), None),
    )
    out_specs = (P(None, None, ("groups", "gx"), None), P("groups", None))
    return jax.shard_map(
        functools.partial(on_device, mesh.shape["gx"]),
        mesh=mesh, in_specs=in_specs, out_specs=out_specs, check_vma=False,
    )
```

time: 357 us -> 309 us (0.87); the launches traced: 353 us -> 309 us
  Pallas kernels: 0 us -> 179 us
  other arithmetic: 86 us -> 0 us
  waiting for transfers between devices: 187 us -> 116 us
  matrix products: 28.6 us -> 0 us
  local copies, waits for them, and re-layouts: 23.1 us -> 0 us
  starting transfers between devices: 12 us -> 0.04 us
    pallas_call x0 -> x3, Pallas kernels: none -> 179 us  [the longest x1 110 us: gather(): pl.pallas_call(functools.partial(gather_kernel, n), out_shape=(jax.ShapeD...]
    all_to_all x1 -> x0, waiting for transfers between devices: 77.5 us -> none  [on_device(): lax.all_to_all(snapshots, 'gx', split_axis=2, concat_axis=0, tiled=True)]
    another operation x9 -> x0, other arithmetic: 54 us -> none  [the longest x6 34 us: make_rotation(): lower_factor = jnp.linalg.cholesky(gram_total)]
    mul x3 -> x0, other arithmetic: 27.4 us -> none  [the longest x2 24.1 us: stencil_apply(): return diffusivity * (along_x + along_y)]
    dot_general x5 -> x0, matrix products: 27.3 us -> none  [the longest x1 11.3 us: on_device(): jnp.einsum('svxy,tvxy->st', snap_float * cell_weights, diffused_raw, prec...]
    unnamed x10 -> x0, local copies, waits for them, and re-layouts: 11.6 us -> none
    all_to_all x1 -> x0, starting transfers between devices: 7.6 us -> none  [on_device(): lax.all_to_all(snapshots, 'gx', split_axis=2, concat_axis=0, tiled=True)]
    psum x1, waiting for transfers between devices: 110 us -> 116 us  [on_device(): gram, cross = lax.psum((gram, cross), 'gx')]
  transfers between devices with their start and end apart: 4 -> 1, of which waited for: 2 -> 1; matrix products, arithmetic and copies ran while one was open for 2% -> 0% of each run, Pallas kernels for 0% -> 0%
where the time goes in v1:
time: 309 us
  Pallas kernels  179 us (58%)
  waiting for transfers between devices  116 us (38%)
  between operations  14 us (5%)
    psum x1, waiting for transfers between devices, on_device(): gram, cross = lax.psum((gram, cross), 'gx')  116 us
    pallas_call x1, Pallas kernels, gather(): pl.pallas_call(functools.partial(gather_kernel, n), out_shape=(jax.ShapeD...  110 us
    pallas_call x1, Pallas kernels, modes(): pl.pallas_call(modes_kernel, out_shape=jax.ShapeDtypeStruct((total, varia...  38.2 us
    pallas_call x1, Pallas kernels, factor(): pl.pallas_call(functools.partial(factor_kernel, float(cells)), out_shape=...  30.3 us
  transfers between devices with their start and end apart: 1, of which 1 were waited for; matrix products, arithmetic and copies ran while one was open for 0% of the time, Pallas kernels for 0%

profile of v1, /device:TPU:0, one launch (start us, length us, event | category | flops | bytes accessed | tf_op | source)
XLA Modules:
  0.0 309.0 jit_solution(11483992448845650101)
XLA Ops:
  7.2 0.0 all-reduce.3.cloned.1.call-start
  7.2 110.2 %gather.1 = (bf16[4,20,256,128]{3,2,1,0:T(8,128)(2,1)}, f32[256,256]{1,0:T(8,128)}, f32[256,256]{1,0:T(8,128)}) custom-call(bf16[16,4,256,128]{3,2,1,0:T(8,128)(2,1)} %snap_ref.1, f32[16,128]{1,0:T(8,128)} %weight_ref.1, f32[4,16,128]{2,1,0:T(8,128)} %diff_ref.3), custom_call_target="tpu_custom_call" | custom-call | tf_op jit(solution)/shard_map/gather/pallas_call | solution.py:199
  117.4 0.0 all-reduce.3.cloned.1.call-update
  117.4 116.2 %all-reduce.3.cloned.1.call-done = (f32[256,256]{1,0:T(8,128)}, f32[256,256]{1,0:T(8,128)}) async-done(((f32[256,256]{1,0:T(8,128)}, f32[256,256]{1,0:T(8,128)}), (f32[256,256]{1,0:T(8,128)}, f32[256,256]{1,0:T(8,128)})) %all-reduce.3.cloned.1.call-update) | async-done | bytes 524304 | tf_op jit(solution)/shard_map/psum | solution.py:347
  233.6 30.3 %factor.1 = (f32[256,256]{1,0:T(8,128)}, f32[256,256]{1,0:T(8,128)}) custom-call(f32[256,256]{1,0:T(8,128)} %get-tuple-element.12.gram_ref, f32[256,256]{1,0:T(8,128)} %get-tuple-element.13.cross_ref), custom_call_target="tpu_custom_call" | custom-call | tf_op jit(solution)/shard_map/factor/pallas_call | solution.py:270
  263.9 38.2 %modes.1 = bf16[256,4,16,128]{3,2,1,0:T(8,128)(2,1)} custom-call(f32[256,256]{1,0:T(8,128)} %get-tuple-element.9.rotation_ref, f32[4,16,128]{2,1,0:T(8,128)} %diff_ref.3, bf16[4,20,256,128]{3,2,1,0:T(8,128)(2,1)} %get-tuple-element.10.x_ref), custom_call_target="tpu_custom_call" | custom-call | tf_op jit(solution)/shard_map/modes/pallas_call | solution.py:326
Async XLA Ops:
  7.2 226.5 %all-reduce.3.cloned.1.call-start = ((), (), s32[]{:S(2)}) async-start(), calls=%async_computation | async-start | bytes 1048576 | tf_op jit(solution)/shard_map/psum | solution.py:347
Sparse Core Ops, SparseCore 0:
  117.5 116.0 all-reduce.2

commit v2 on v1

v2 whole, which is shorter than its diff:
```python
import functools

import jax
import jax.numpy as jnp
from jax import lax
from jax.experimental import pallas as pl
from jax.experimental.pallas import tpu as pltpu
from jax.sharding import PartitionSpec as P

MESH = pl.DeviceIdType.MESH
HIGHEST = lax.Precision.HIGHEST
NT = (((1,), (1,)), ((), ()))
TN = (((0,), (0,)), ((), ()))
PACK = 16
PIVOTS = 32
PANEL = 8


def iota(shape, dim):
    return lax.broadcasted_iota(jnp.int32, shape, dim)


def swap_matrix(outer, inner):
    size = outer * inner
    row, col = iota((size, size), 0), iota((size, size), 1)
    source = lax.rem(row, inner) * outer + lax.div(row, inner)
    return jnp.where(col == source, 1.0, 0.0).astype(jnp.bfloat16)


def parts_of(value, count):
    parts = []
    for _ in range(count):
        part = value.astype(jnp.bfloat16)
        parts.append(part)
        value = value - part.astype(jnp.float32)
    return parts


def dot32(a, b, dims):
    return lax.dot_general(a, b, dims, preferred_element_type=jnp.float32)


NN = (((1,), (0,)), ((), ()))


def gather_kernel(n, snap_ref, weight_ref, diff_ref, x_ref, sums_ref,
                  pod, parts, part_sums, half, pieces,
                  local_sem, send_sem, recv_sem, halo_send, halo_recv, sum_send, sum_recv):
    me = lax.axis_index("gx")
    own, variables, _, cols = snap_ref.shape
    total, rows = pod.shape[0], pod.shape[2]
    gram_ref, cross_ref = part_sums.at[0], part_sums.at[1]

    barrier = pltpu.get_barrier_semaphore()

    def greet(k, carry):
        pl.semaphore_signal(
            barrier, inc=1, device_id={"gx": lax.rem(me + k, n)}, device_id_type=MESH
        )
        return carry

    lax.fori_loop(1, n, greet, 0)

    def own_copy(v):
        return pltpu.make_async_copy(
            snap_ref.at[:, v, pl.ds(me * rows, rows)],
            pod.at[pl.ds(me * own, own), v],
            local_sem.at[v],
        )

    def send_all(v):
        def send(k, carry):
            offset = lax.div(k, 2) + lax.rem(k, 2) * (n // 2)
            target = lax.rem(me + offset, n)
            pltpu.make_async_remote_copy(
                src_ref=snap_ref.at[:, v, pl.ds(target * rows, rows)],
                dst_ref=pod.at[pl.ds(me * own, own), v],
                send_sem=send_sem.at[v],
                recv_sem=recv_sem.at[v],
                device_id={"gx": target},
                device_id_type=MESH,
            ).start()
            return carry

        lax.fori_loop(1, n, send, 0)

    for v in range(variables):
        own_copy(v).start()
    pl.semaphore_wait(barrier, n - 1)
    ahead = min(2, variables)
    for v in range(ahead):
        send_all(v)

    part_sums[...] = jnp.zeros_like(part_sums)
    lane_gap = iota((cols, cols), 0) - iota((cols, cols), 1)
    band = jnp.where(lane_gap == 0, -60.0, 0.0)
    band = jnp.where(jnp.abs(lane_gap) == 1, 16.0, band)
    band = jnp.where(jnp.abs(lane_gap) == 2, -1.0, band).astype(jnp.bfloat16)
    swap = swap_matrix(rows, PACK)

    def all_but_own(v, sem):
        piece = pod.at[pl.ds(0, total - own), v]
        return pltpu.make_async_copy(piece, piece, sem.at[v])

    def strip(v, first, count):
        return x_ref.at[v, :, pl.ds(first * cols, count * cols)]

    def to_low(v):
        return pltpu.make_async_remote_copy(
            src_ref=strip(v, 2, 2),
            dst_ref=strip(v, rows + 2, 2),
            send_sem=halo_send.at[0, v],
            recv_sem=halo_recv.at[0, v],
            device_id={"gx": jnp.maximum(me - 1, 0)},
            device_id_type=MESH,
        )

    def to_high(v):
        return pltpu.make_async_remote_copy(
            src_ref=strip(v, rows, 2),
            dst_ref=strip(v, 0, 2),
            send_sem=halo_send.at[1, v],
            recv_sem=halo_recv.at[1, v],
            device_id={"gx": jnp.minimum(me + 1, n - 1)},
            device_id_type=MESH,
        )

    def relayout(v):
        for g in range(0, total // PACK, 2):
            blocks = [
                pod[PACK * (g + h) : PACK * (g + h + 1), v].reshape(PACK * rows, cols)
                for h in range(2)
            ]
            turned = dot32(swap, jnp.concatenate(blocks, axis=1), NN).astype(jnp.bfloat16)
            for h in range(2):
                for at in range(rows):
                    x_ref[v, PACK * (g + h) : PACK * (g + h + 1), (at + 2) * cols : (at + 3) * cols] = (
                        turned[at * PACK : (at + 1) * PACK, h * cols : (h + 1) * cols]
                    )

    def accumulate(v, acc_ref):
        left = x_ref[v, :, 2 * cols : (rows + 2) * cols]
        acc = acc_ref[...]
        for p in range(3):
            acc += dot32(left, parts[p], NT)
        acc_ref[...] = acc

    def store_parts(at, value):
        for p, part in enumerate(parts_of(value, 3)):
            parts[p, :, at * cols : (at + 1) * cols] = part

    def gram(v):
        for at in range(rows):
            field = x_ref[v, :, (at + 2) * cols : (at + 3) * cols].astype(jnp.float32)
            store_parts(at, field * weight_ref[at : at + 1, :])
        accumulate(v, gram_ref)

    def cross(v):
        @pl.when(me < n - 1)
        def _():
            to_low(v).wait_recv()
            to_high(v).wait_send()

        @pl.when(me > 0)
        def _():
            to_high(v).wait_recv()
            to_low(v).wait_send()

        for at in range(rows):
            near = [x_ref[v, :, (at + k) * cols : (at + k + 1) * cols] for k in range(5)]
            wide = [near[k].astype(jnp.float32) for k in (0, 1, 3, 4)]
            spread = dot32(near[2], band, NN)
            spread += 16.0 * (wide[1] + wide[2]) - (wide[0] + wide[3])
            scale = weight_ref[at : at + 1, :] * diff_ref[v, at : at + 1, :]
            store_parts(at, spread * (scale / 12.0))
        accumulate(v, cross_ref)

    @pl.loop(0, variables)
    def _(v):
        own_copy(v).wait()
        all_but_own(v, recv_sem).wait()
        relayout(v)

        @pl.when(me > 0)
        def _():
            to_low(v).start()

        @pl.when(me < n - 1)
        def _():
            to_high(v).start()

        @pl.when(me == 0)
        def _():
            x_ref[v, :, : 2 * cols] = jnp.zeros((total, 2 * cols), jnp.bfloat16)

        @pl.when(me == n - 1)
        def _():
            x_ref[v, :, (rows + 2) * cols :] = jnp.zeros((total, 2 * cols), jnp.bfloat16)

        @pl.when(v + ahead < variables)
        def _():
            send_all(v + ahead)

        @pl.when(v > 0)
        def _():
            cross(v - 1)

        gram(v)

    cross(variables - 1)

    core, chip, chips = lax.rem(me, 2), lax.div(me, 2), n // 2
    share = total // chips
    partner = me + 1 - 2 * core

    def remote(source, target, stage, device):
        return pltpu.make_async_remote_copy(
            src_ref=source,
            dst_ref=target,
            send_sem=sum_send.at[stage],
            recv_sem=sum_recv.at[stage],
            device_id={"gx": device},
            device_id_type=MESH,
        )

    swapped = remote(part_sums.at[1 - core], half, 0, partner)
    swapped.start()
    swapped.wait()
    half[...] += part_sums[core]

    def peer(k):
        return lax.rem(chip + k, chips)

    def scatter(k, carry):
        remote(half.at[pl.ds(peer(k) * share, share)], pieces.at[k - 1], 1, 2 * peer(k) + core).start()
        return carry

    lax.fori_loop(1, chips, scatter, 0)
    remote(pieces, pieces, 1, partner).wait()
    mine = pl.ds(pl.multiple_of(chip * share, share), share)
    acc = half[mine, :]
    for k in range(chips - 1):
        acc += pieces[k]
    sums_ref[core, mine, :] = acc

    def spread_out(k, carry):
        piece = sums_ref.at[core, mine]
        remote(piece, piece, 2, 2 * peer(k) + core).start()
        return carry

    lax.fori_loop(1, chips, spread_out, 0)
    others = sums_ref.at[core, pl.ds(0, total - share)]
    remote(others, others, 2, partner).wait()
    final = remote(sums_ref.at[core], sums_ref.at[core], 3, partner)
    final.start()
    final.wait_send()
    remote(sums_ref.at[1 - core], sums_ref.at[1 - core], 3, partner).wait_recv()

    for v in range(variables):
        all_but_own(v, send_sem).wait()


def gather(n, snapshots, cell_weights, diffusivity):
    own, variables, _, cols = snapshots.shape
    rows = cell_weights.shape[0]
    total = own * n
    vmem = pl.BlockSpec(memory_space=pltpu.VMEM)
    chips = n // 2
    dma = pltpu.SemaphoreType.DMA
    return pl.pallas_call(
        functools.partial(gather_kernel, n),
        out_shape=(
            jax.ShapeDtypeStruct((variables, total, (rows + 4) * cols), jnp.bfloat16),
            jax.ShapeDtypeStruct((2, total, total), jnp.float32),
        ),
        in_specs=[pl.BlockSpec(memory_space=pl.ANY), vmem, vmem],
        out_specs=(vmem, vmem),
        scratch_shapes=[
            pltpu.VMEM((total, variables, rows, cols), jnp.bfloat16),
            pltpu.VMEM((3, total, rows * cols), jnp.bfloat16),
            pltpu.VMEM((2, total, total), jnp.float32),
            pltpu.VMEM((total, total), jnp.float32),
            pltpu.VMEM((chips - 1, total // chips, total), jnp.float32),
            dma((variables,)),
            dma((variables,)),
            dma((variables,)),
            dma((2, variables)),
            dma((2, variables)),
            dma((4,)),
            dma((4,)),
        ],
        compiler_params=pltpu.CompilerParams(collective_id=0, has_side_effects=True),
        name="gather",
    )(snapshots, cell_weights, diffusivity)


def factor_kernel(cells, sums_ref, rotation_ref, reduced_ref, work):
    size = sums_ref.shape[1]
    lanes = 128
    work[:, :size] = sums_ref[0] * (1.0 / cells)
    work[:, size:] = jnp.where(iota((size, size), 0) == iota((size, size), 1), 1.0, 0.0)
    rotation_ref[...] = jnp.zeros_like(rotation_ref)
    row = iota((PIVOTS, lanes), 0)
    lane = iota((PIVOTS, lanes), 1)
    for first in range(0, size, PIVOTS):
        last = first + PIVOTS
        group, shift = first // lanes * lanes, first % lanes
        stop = size + group + lanes
        block = work[first:last, group : group + lanes]
        if shift:
            block = pltpu.roll(block, lanes - shift, 1)
        block = jnp.where(lane < PIVOTS, block, jnp.where(lane == row + PIVOTS, 1.0, 0.0))
        for base in range(0, PIVOTS, PANEL):
            columns = [
                jnp.broadcast_to(block[:, k : k + 1], (PIVOTS, lanes))
                for k in range(base, base + PANEL)
            ]
            for j in range(PANEL):
                k = base + j
                factor_of = jnp.where(row > k, columns[j] * (1.0 / columns[j][k : k + 1, :]), 0.0)
                for i in range(j + 1, PANEL):
                    columns[i] = columns[i] - factor_of * columns[i][k : k + 1, :]
                block = block - factor_of * block[k : k + 1, :]
        pivots = jnp.sum(jnp.where(lane == row, block, 0.0), axis=1, keepdims=True)
        inverse = pltpu.roll(block, lanes - PIVOTS, 1) / jnp.sqrt(pivots)
        stripe = jnp.dot(
            inverse[:, :PIVOTS],
            work[first:last, group:stop],
            precision=HIGHEST,
            preferred_element_type=jnp.float32,
        )
        rotation_ref[first:last, : group + lanes] = stripe[:, size - group :]
        if last < size:
            low = last // lanes * lanes
            work[low:, group:stop] -= lax.dot_general(
                stripe[:, low - group : size - group],
                stripe,
                TN,
                precision=HIGHEST,
                preferred_element_type=jnp.float32,
            )
    rotation = rotation_ref[...]
    turned = jnp.dot(
        rotation, sums_ref[1] * (1.0 / cells), precision=HIGHEST,
        preferred_element_type=jnp.float32,
    )
    reduced_ref[...] = lax.dot_general(
        turned, rotation, NT, precision=HIGHEST, preferred_element_type=jnp.float32
    )


def factor(cells, sums):
    size = sums.shape[1]
    vmem = pl.BlockSpec(memory_space=pltpu.VMEM)
    square = jax.ShapeDtypeStruct((size, size), jnp.float32)
    return pl.pallas_call(
        functools.partial(factor_kernel, float(cells)),
        out_shape=(square, square),
        in_specs=[vmem],
        out_specs=(vmem, vmem),
        scratch_shapes=[pltpu.VMEM((size, 2 * size), jnp.float32)],
        name="factor",
    )(sums)


def modes_kernel(rotation_ref, diff_ref, x_ref, out_ref, field, turned):
    rows, cols = diff_ref.shape[1:]
    total = rotation_ref.shape[0]
    parts = parts_of(rotation_ref[...], 3)
    lane = iota((1, cols), 1)
    masks = {
        shift: jnp.where(
            (lane >= shift) & (lane < cols + shift), -1.0 if abs(shift) == 2 else 16.0, 0.0
        )
        for shift in (-2, -1, 1, 2)
    }
    for at in range(0, (rows + 4) * cols, 2 * cols):
        right = x_ref[0, :, at : at + 2 * cols]
        acc = dot32(parts[0], right, NN)
        for part in parts[1:]:
            acc += dot32(part, right, NN)
        field[:, at : at + 2 * cols] = acc

    for at in range(rows):
        near = [field[:, (at + k) * cols : (at + k + 1) * cols] for k in range(5)]
        spread = 16.0 * (near[1] + near[3]) - (near[0] + near[4]) - 60.0 * near[2]
        for shift in (-2, -1, 1, 2):
            spread += pltpu.roll(near[2], shift % cols, 1) * masks[shift]
        spread = spread * (diff_ref[0, at : at + 1, :] / 12.0)
        turned[at] = spread.astype(jnp.bfloat16)

    swap = swap_matrix(PACK, rows)
    for g in range(0, total // PACK, 2):
        blocks = [
            turned[:, PACK * (g + h) : PACK * (g + h + 1), :].reshape(rows * PACK, cols)
            for h in range(2)
        ]
        done = dot32(swap, jnp.concatenate(blocks, axis=1), NN).astype(jnp.bfloat16)
        for h in range(2):
            out_ref[PACK * (g + h) : PACK * (g + h + 1), 0] = done[
                :, h * cols : (h + 1) * cols
            ].reshape(PACK, rows, cols)


def modes(rotation, diffusivity, fields):
    variables, rows, cols = diffusivity.shape
    total = rotation.shape[0]
    return pl.pallas_call(
        modes_kernel,
        out_shape=jax.ShapeDtypeStruct((total, variables, rows, cols), jnp.bfloat16),
        grid=(variables,),
        in_specs=[
            pl.BlockSpec((total, total), lambda v: (0, 0)),
            pl.BlockSpec((1, rows, cols), lambda v: (v, 0, 0)),
            pl.BlockSpec((1, total, (rows + 4) * cols), lambda v: (v, 0, 0)),
        ],
        out_specs=pl.BlockSpec((total, 1, rows, cols), lambda v: (0, v, 0, 0)),
        scratch_shapes=[
            pltpu.VMEM((total, (rows + 4) * cols), jnp.float32),
            pltpu.VMEM((rows, total, cols), jnp.bfloat16),
        ],
        name="modes",
    )(rotation, diffusivity, fields)


def on_device(n, snapshots, cell_weights, diffusivity):
    variables, rows, cols = diffusivity.shape
    fields, sums = gather(n, snapshots, cell_weights, diffusivity)
    rotation, reduced = factor(variables * rows * cols * n, sums)
    return modes(rotation, diffusivity, fields), reduced


def solution(mesh):
    in_specs = (
        P("gx", None, "groups", None),
        P(("groups", "gx"), None),
        P(None, ("groups", "gx"), None),
    )
    out_specs = (P(None, None, ("groups", "gx"), None), P("groups", None))
    return jax.shard_map(
        functools.partial(on_device, mesh.shape["gx"]),
        mesh=mesh, in_specs=in_specs, out_specs=out_specs, check_vma=False,
    )
```

time: 309 us -> 157 us (0.51)
  waiting for transfers between devices: 116 us -> 0 us
  Pallas kernels: 179 us -> 155 us
  between operations: 14 us -> 0.64 us
    psum x1 -> x0, waiting for transfers between devices: 116 us -> none  [on_device(): gram, cross = lax.psum((gram, cross), 'gx')]
    pallas_call x1, Pallas kernels: 38.2 us -> 14.4 us  [modes(): pl.pallas_call(modes_kernel, out_shape=jax.ShapeDtypeStruct((total, varia...]
    pallas_call x1, Pallas kernels: 110 us -> 126 us  [gather(): pl.pallas_call(functools.partial(gather_kernel, n), out_shape=(jax.ShapeD...]
    pallas_call x1, Pallas kernels: 30.3 us -> 14.4 us  [factor(): pl.pallas_call(functools.partial(factor_kernel, float(cells)), out_shape=...]
  transfers between devices with their start and end apart: 1 -> 0, of which waited for: 1 -> 0; matrix products, arithmetic and copies ran while one was open for 0% -> 0% of each run, Pallas kernels for 0% -> 0%
where the time goes in v2:
time: 157 us; the launch traced here: 156 us
  Pallas kernels  155 us (99%)
    pallas_call x1, Pallas kernels, gather(): pl.pallas_call(functools.partial(gather_kernel, n), out_shape=(jax.ShapeD...  126 us
    pallas_call x1, Pallas kernels, factor(): pl.pallas_call(functools.partial(factor_kernel, float(cells)), out_shape=...  14.4 us
    pallas_call x1, Pallas kernels, modes(): pl.pallas_call(modes_kernel, out_shape=jax.ShapeDtypeStruct((total, varia...  14.4 us

profile of v2, /device:TPU:0, one launch (start us, length us, event | category | flops | bytes accessed | tf_op | source)
XLA Modules:
  0.0 155.6 jit_solution(12635041447258038695)
XLA Ops:
  0.6 126.1 %gather.1 = (bf16[4,256,2560]{2,1,0:T(8,128)(2,1)}, f32[2,256,256]{2,1,0:T(8,128)}) custom-call(bf16[16,4,256,128]{3,2,1,0:T(8,128)(2,1)} %snap_ref.1, f32[16,128]{1,0:T(8,128)} %weight_ref.1, f32[4,16,128]{2,1,0:T(8,128)} %diff_ref.3), custom_call_target="tpu_custom_call" | custom-call | tf_op jit(solution)/shard_map/gather/pallas_call | solution.py:270
  126.8 14.4 %factor.1 = (f32[256,256]{1,0:T(8,128)}, f32[256,256]{1,0:T(8,128)}) custom-call(f32[2,256,256]{2,1,0:T(8,128)} %get-tuple-element.6.sums_ref), custom_call_target="tpu_custom_call" | custom-call | tf_op jit(solution)/shard_map/factor/pallas_call | solution.py:356
  141.2 14.4 %modes.1 = bf16[256,4,16,128]{3,2,1,0:T(8,128)(2,1)} custom-call(f32[256,256]{1,0:T(8,128)} %get-tuple-element.7.rotation_ref, f32[4,16,128]{2,1,0:T(8,128)} %diff_ref.3, bf16[4,256,2560]{2,1,0:T(8,128)(2,1)} %get-tuple-element.8.x_ref), custom_call_target="tpu_custom_call" | custom-call | tf_op jit(solution)/shard_map/modes/pallas_call | solution.py:408

commit v3 on v2

--- a/solution.py
+++ b/solution.py
@@ -43,13 +43,12 @@
 NN = (((1,), (0,)), ((), ()))
 
 
-def gather_kernel(n, snap_ref, weight_ref, diff_ref, x_ref, sums_ref,
-                  pod, parts, part_sums, half, pieces,
-                  local_sem, send_sem, recv_sem, halo_send, halo_recv, sum_send, sum_recv):
+def gather_kernel(n, cells, snap_ref, weight_ref, diff_ref, field_ref, sums_ref, rotation_ref,
+                  pod, x_ref, parts, part_sums, half, pieces, work, local_sem, out_sem,
+                  send_sem, recv_sem, halo_send, halo_recv, sum_send, sum_recv):
     me = lax.axis_index("gx")
     own, variables, _, cols = snap_ref.shape
     total, rows = pod.shape[0], pod.shape[2]
-    gram_ref, cross_ref = part_sums.at[0], part_sums.at[1]
 
     barrier = pltpu.get_barrier_semaphore()
 
@@ -67,6 +66,9 @@
             pod.at[pl.ds(me * own, own), v],
             local_sem.at[v],
         )
+
+    def out_copy(v):
+        return pltpu.make_async_copy(x_ref.at[v], field_ref.at[v], out_sem.at[v])
 
     def send_all(v):
         def send(k, carry):
@@ -138,12 +140,13 @@
                         turned[at * PACK : (at + 1) * PACK, h * cols : (h + 1) * cols]
                     )
 
-    def accumulate(v, acc_ref):
+    def accumulate(v, which):
         left = x_ref[v, :, 2 * cols : (rows + 2) * cols]
-        acc = acc_ref[...]
-        for p in range(3):
+        acc = dot32(left, parts[0], NT)
+        for p in range(1, 3):
             acc += dot32(left, parts[p], NT)
-        acc_ref[...] = acc
+        part_sums[which, 0] += acc[:, : total // 2]
+        part_sums[which, 1] += acc[:, total // 2 :]
 
     def store_parts(at, value):
         for p, part in enumerate(parts_of(value, 3)):
@@ -153,7 +156,7 @@
         for at in range(rows):
             field = x_ref[v, :, (at + 2) * cols : (at + 3) * cols].astype(jnp.float32)
             store_parts(at, field * weight_ref[at : at + 1, :])
-        accumulate(v, gram_ref)
+        accumulate(v, 0)
 
     def cross(v):
         @pl.when(me < n - 1)
@@ -173,7 +176,8 @@
             spread += 16.0 * (wide[1] + wide[2]) - (wide[0] + wide[3])
             scale = weight_ref[at : at + 1, :] * diff_ref[v, at : at + 1, :]
             store_parts(at, spread * (scale / 12.0))
-        accumulate(v, cross_ref)
+        accumulate(v, 1)
+        out_copy(v).start()
 
     @pl.loop(0, variables)
     def _(v):
@@ -201,103 +205,97 @@
         def _():
             send_all(v + ahead)
 
-        @pl.when(v > 0)
+        @pl.when((v > 0) & (v < variables - 1))
         def _():
             cross(v - 1)
 
         gram(v)
-
-    cross(variables - 1)
 
     core, chip, chips = lax.rem(me, 2), lax.div(me, 2), n // 2
     share = total // chips
     partner = me + 1 - 2 * core
 
-    def remote(source, target, stage, device):
+    mine = pl.ds(pl.multiple_of(chip * share, share), share)
+
+    def remote(source, target, which, stage, device):
         return pltpu.make_async_remote_copy(
             src_ref=source,
             dst_ref=target,
-            send_sem=sum_send.at[stage],
-            recv_sem=sum_recv.at[stage],
+            send_sem=sum_send.at[which, stage],
+            recv_sem=sum_recv.at[which, stage],
             device_id={"gx": device},
             device_id_type=MESH,
         )
 
-    swapped = remote(part_sums.at[1 - core], half, 0, partner)
-    swapped.start()
-    swapped.wait()
-    half[...] += part_sums[core]
-
     def peer(k):
         return lax.rem(chip + k, chips)
 
-    def scatter(k, carry):
-        remote(half.at[pl.ds(peer(k) * share, share)], pieces.at[k - 1], 1, 2 * peer(k) + core).start()
-        return carry
-
-    lax.fori_loop(1, chips, scatter, 0)
-    remote(pieces, pieces, 1, partner).wait()
-    mine = pl.ds(pl.multiple_of(chip * share, share), share)
-    acc = half[mine, :]
-    for k in range(chips - 1):
-        acc += pieces[k]
-    sums_ref[core, mine, :] = acc
-
-    def spread_out(k, carry):
-        piece = sums_ref.at[core, mine]
-        remote(piece, piece, 2, 2 * peer(k) + core).start()
-        return carry
-
-    lax.fori_loop(1, chips, spread_out, 0)
-    others = sums_ref.at[core, pl.ds(0, total - share)]
-    remote(others, others, 2, partner).wait()
-    final = remote(sums_ref.at[core], sums_ref.at[core], 3, partner)
-    final.start()
-    final.wait_send()
-    remote(sums_ref.at[1 - core], sums_ref.at[1 - core], 3, partner).wait_recv()
+    def pair_up(which):
+        return remote(part_sums.at[which, 1 - core], half.at[which], which, 0, partner)
+
+    def scatter(which):
+        pair_up(which).wait()
+        half[which] += part_sums[which, core]
+
+        def send(k, carry):
+            piece = half.at[which, pl.ds(peer(k) * share, share)]
+            remote(piece, pieces.at[which, k - 1], which, 1, 2 * peer(k) + core).start()
+            return carry
+
+        lax.fori_loop(1, chips, send, 0)
+
+    def spread_out(which):
+        remote(pieces.at[which], pieces.at[which], which, 1, partner).wait()
+        acc = half[which, mine, :]
+        for k in range(chips - 1):
+            acc += pieces[which, k]
+        sums_ref[which, core, mine, :] = acc
+
+        def send(k, carry):
+            piece = sums_ref.at[which, core, mine]
+            remote(piece, piece, which, 2, 2 * peer(k) + core).start()
+            return carry
+
+        lax.fori_loop(1, chips, send, 0)
+
+    def hand_over(which):
+        others = sums_ref.at[which, core, pl.ds(0, total - share)]
+        remote(others, others, which, 2, partner).wait()
+        done = sums_ref.at[which, core]
+        remote(done, done, which, 3, partner).start()
+
+    def finish(which):
+        sent, got = sums_ref.at[which, core], sums_ref.at[which, 1 - core]
+        remote(sent, sent, which, 3, partner).wait_send()
+        remote(got, got, which, 3, partner).wait_recv()
+
+    pair_up(0).start()
+    if variables > 1:
+        cross(variables - 2)
+    scatter(0)
+    cross(variables - 1)
+    pair_up(1).start()
+    spread_out(0)
+    hand_over(0)
+    finish(0)
+
+    stages = {1: scatter, 3: spread_out, 5: hand_over, 7: finish}
+    for step in factor(cells, sums_ref, rotation_ref, work):
+        if step in stages:
+            stages.pop(step)(1)
+    for stage in stages.values():
+        stage(1)
 
     for v in range(variables):
+        out_copy(v).wait()
         all_but_own(v, send_sem).wait()
 
 
-def gather(n, snapshots, cell_weights, diffusivity):
-    own, variables, _, cols = snapshots.shape
-    rows = cell_weights.shape[0]
-    total = own * n
-    vmem = pl.BlockSpec(memory_space=pltpu.VMEM)
-    chips = n // 2
-    dma = pltpu.SemaphoreType.DMA
-    return pl.pallas_call(
-        functools.partial(gather_kernel, n),
-        out_shape=(
-            jax.ShapeDtypeStruct((variables, total, (rows + 4) * cols), jnp.bfloat16),
-            jax.ShapeDtypeStruct((2, total, total), jnp.float32),
-        ),
-        in_specs=[pl.BlockSpec(memory_space=pl.ANY), vmem, vmem],
-        out_specs=(vmem, vmem),
-        scratch_shapes=[
-            pltpu.VMEM((total, variables, rows, cols), jnp.bfloat16),
-            pltpu.VMEM((3, total, rows * cols), jnp.bfloat16),
-            pltpu.VMEM((2, total, total), jnp.float32),
-            pltpu.VMEM((total, total), jnp.float32),
-            pltpu.VMEM((chips - 1, total // chips, total), jnp.float32),
-            dma((variables,)),
-            dma((variables,)),
-            dma((variables,)),
-            dma((2, variables)),
-            dma((2, variables)),
-            dma((4,)),
-            dma((4,)),
-        ],
-        compiler_params=pltpu.CompilerParams(collective_id=0, has_side_effects=True),
-        name="gather",
-    )(snapshots, cell_weights, diffusivity)
-
-
-def factor_kernel(cells, sums_ref, rotation_ref, reduced_ref, work):
-    size = sums_ref.shape[1]
+def factor(cells, sums_ref, rotation_ref, work):
+    size = rotation_ref.shape[0]
     lanes = 128
-    work[:, :size] = sums_ref[0] * (1.0 / cells)
+    work[:, : size // 2] = sums_ref[0, 0] * (1.0 / cells)
+    work[:, size // 2 : size] = sums_ref[0, 1] * (1.0 / cells)
     work[:, size:] = jnp.where(iota((size, size), 0) == iota((size, size), 1), 1.0, 0.0)
     rotation_ref[...] = jnp.zeros_like(rotation_ref)
     row = iota((PIVOTS, lanes), 0)
@@ -339,34 +337,63 @@
                 precision=HIGHEST,
                 preferred_element_type=jnp.float32,
             )
-    rotation = rotation_ref[...]
-    turned = jnp.dot(
-        rotation, sums_ref[1] * (1.0 / cells), precision=HIGHEST,
-        preferred_element_type=jnp.float32,
-    )
-    reduced_ref[...] = lax.dot_general(
-        turned, rotation, NT, precision=HIGHEST, preferred_element_type=jnp.float32
-    )
-
-
-def factor(cells, sums):
-    size = sums.shape[1]
+        yield first // PIVOTS
+
+
+def gather(n, cells, snapshots, cell_weights, diffusivity):
+    own, variables, _, cols = snapshots.shape
+    rows = cell_weights.shape[0]
+    total = own * n
     vmem = pl.BlockSpec(memory_space=pltpu.VMEM)
-    square = jax.ShapeDtypeStruct((size, size), jnp.float32)
+    chips = n // 2
+    dma = pltpu.SemaphoreType.DMA
     return pl.pallas_call(
-        functools.partial(factor_kernel, float(cells)),
-        out_shape=(square, square),
-        in_specs=[vmem],
-        out_specs=(vmem, vmem),
-        scratch_shapes=[pltpu.VMEM((size, 2 * size), jnp.float32)],
-        name="factor",
-    )(sums)
-
-
-def modes_kernel(rotation_ref, diff_ref, x_ref, out_ref, field, turned):
+        functools.partial(gather_kernel, n, float(cells)),
+        out_shape=(
+            jax.ShapeDtypeStruct((variables, total, (rows + 4) * cols), jnp.bfloat16),
+            jax.ShapeDtypeStruct((2, 2, total, total // 2), jnp.float32),
+            jax.ShapeDtypeStruct((total, total), jnp.float32),
+        ),
+        in_specs=[pl.BlockSpec(memory_space=pl.ANY), vmem, vmem],
+        out_specs=(pl.BlockSpec(memory_space=pl.ANY), vmem, vmem),
+        scratch_shapes=[
+            pltpu.VMEM((total, variables, rows, cols), jnp.bfloat16),
+            pltpu.VMEM((variables, total, (rows + 4) * cols), jnp.bfloat16),
+            pltpu.VMEM((3, total, rows * cols), jnp.bfloat16),
+            pltpu.VMEM((2, 2, total, total // 2), jnp.float32),
+            pltpu.VMEM((2, total, total // 2), jnp.float32),
+            pltpu.VMEM((2, chips - 1, total // chips, total // 2), jnp.float32),
+            pltpu.VMEM((total, 2 * total), jnp.float32),
+            dma((variables,)),
+            dma((variables,)),
+            dma((variables,)),
+            dma((variables,)),
+            dma((2, variables)),
+            dma((2, variables)),
+            dma((2, 4)),
+            dma((2, 4)),
+        ],
+        compiler_params=pltpu.CompilerParams(collective_id=0, has_side_effects=True),
+        name="gather",
+    )(snapshots, cell_weights, diffusivity)
+
+
+def modes_kernel(cells, rotation_ref, sums_ref, diff_ref, x_ref, out_ref, reduced_ref, field, turned):
     rows, cols = diff_ref.shape[1:]
     total = rotation_ref.shape[0]
     parts = parts_of(rotation_ref[...], 3)
+
+    @pl.when(pl.program_id(0) == 0)
+    def _():
+        rotation = rotation_ref[...]
+        cross = jnp.concatenate([sums_ref[0, 0], sums_ref[0, 1]], axis=1) * (1.0 / cells)
+        product = jnp.dot(
+            rotation, cross, precision=HIGHEST, preferred_element_type=jnp.float32
+        )
+        reduced_ref[...] = lax.dot_general(
+            product, rotation, NT, precision=HIGHEST, preferred_element_type=jnp.float32
+        )
+
     lane = iota((1, cols), 1)
     masks = {
         shift: jnp.where(
@@ -402,32 +429,39 @@
             ].reshape(PACK, rows, cols)
 
 
-def modes(rotation, diffusivity, fields):
+def modes(cells, rotation, sums, diffusivity, fields):
     variables, rows, cols = diffusivity.shape
     total = rotation.shape[0]
     return pl.pallas_call(
-        modes_kernel,
-        out_shape=jax.ShapeDtypeStruct((total, variables, rows, cols), jnp.bfloat16),
+        functools.partial(modes_kernel, float(cells)),
+        out_shape=(
+            jax.ShapeDtypeStruct((total, variables, rows, cols), jnp.bfloat16),
+            jax.ShapeDtypeStruct((total, total), jnp.float32),
+        ),
         grid=(variables,),
         in_specs=[
             pl.BlockSpec((total, total), lambda v: (0, 0)),
+            pl.BlockSpec((1, 2, total, total // 2), lambda v: (1, 0, 0, 0)),
             pl.BlockSpec((1, rows, cols), lambda v: (v, 0, 0)),
             pl.BlockSpec((1, total, (rows + 4) * cols), lambda v: (v, 0, 0)),
         ],
-        out_specs=pl.BlockSpec((total, 1, rows, cols), lambda v: (0, v, 0, 0)),
+        out_specs=(
+            pl.BlockSpec((total, 1, rows, cols), lambda v: (0, v, 0, 0)),
+            pl.BlockSpec((total, total), lambda v: (0, 0)),
+        ),
         scratch_shapes=[
             pltpu.VMEM((total, (rows + 4) * cols), jnp.float32),
             pltpu.VMEM((rows, total, cols), jnp.bfloat16),
         ],
         name="modes",
-    )(rotation, diffusivity, fields)
+    )(rotation, sums, diffusivity, fields)
 
 
 def on_device(n, snapshots, cell_weights, diffusivity):
     variables, rows, cols = diffusivity.shape
-    fields, sums = gather(n, snapshots, cell_weights, diffusivity)
-    rotation, reduced = factor(variables * rows * cols * n, sums)
-    return modes(rotation, diffusivity, fields), reduced
+    cells = variables * rows * cols * n
+    fields, sums, rotation = gather(n, cells, snapshots, cell_weights, diffusivity)
+    return modes(cells, rotation, sums, diffusivity, fields)
 
 
 def solution(mesh):

time: 157 us -> 150 us (0.955)
  Pallas kernels: 155 us -> 149 us
    pallas_call x3 -> x2, Pallas kernels: 155 us -> 149 us  [the longest x1 133 us: gather(): pl.pallas_call(functools.partial(gather_kernel, n, float(cells)), out_sha...]
where the time goes in v3:
time: 150 us
  Pallas kernels  149 us (99%)
    pallas_call x1, Pallas kernels, gather(): pl.pallas_call(functools.partial(gather_kernel, n, float(cells)), out_sha...  133 us
    pallas_call x1, Pallas kernels, modes(): pl.pallas_call(functools.partial(modes_kernel, float(cells)), out_shape=(...  15.9 us

profile of v3, /device:TPU:0, one launch (start us, length us, event | category | flops | bytes accessed | tf_op | source)
XLA Modules:
  0.0 149.8 jit_solution(5340940416706559788)
XLA Ops:
  0.6 133.2 %gather.1 = (bf16[4,256,2560]{2,1,0:T(8,128)(2,1)}, f32[2,2,256,128]{3,2,1,0:T(8,128)}, f32[256,256]{1,0:T(8,128)}) custom-call(bf16[16,4,256,128]{3,2,1,0:T(8,128)(2,1)} %snap_ref.1, f32[16,128]{1,0:T(8,128)} %weight_ref.1, f32[4,16,128]{2,1,0:T(8,128)} %diff_ref.3), custom_call_target="tpu_custom_call" | custom-call | tf_op jit(solution)/shard_map/gather/pallas_call | solution.py:350
  133.9 15.9 %modes.1 = (bf16[256,4,16,128]{3,2,1,0:T(8,128)(2,1)}, f32[256,256]{1,0:T(8,128)}) custom-call(f32[256,256]{1,0:T(8,128)} %get-tuple-element.5.rotation_ref, f32[2,2,256,128]{3,2,1,0:T(8,128)} %get-tuple-element.6.sums_ref, f32[4,16,128]{2,1,0:T(8,128)} %diff_ref.3, bf16[4,256,2560]{2,1,0:T(8,128)(2,1)} %get-tuple-element.7.x_ref), custom_call_target="tpu_custom_call" | custom-call | tf_op jit(solution)/shard_map/modes/pallas_call | solution.py:435

commit v4 on v3

--- a/solution.py
+++ b/solution.py
@@ -140,23 +140,23 @@
                         turned[at * PACK : (at + 1) * PACK, h * cols : (h + 1) * cols]
                     )
 
-    def accumulate(v, which):
+    def accumulate(v, which, count):
         left = x_ref[v, :, 2 * cols : (rows + 2) * cols]
         acc = dot32(left, parts[0], NT)
-        for p in range(1, 3):
+        for p in range(1, count):
             acc += dot32(left, parts[p], NT)
         part_sums[which, 0] += acc[:, : total // 2]
         part_sums[which, 1] += acc[:, total // 2 :]
 
-    def store_parts(at, value):
-        for p, part in enumerate(parts_of(value, 3)):
+    def store_parts(at, value, count):
+        for p, part in enumerate(parts_of(value, count)):
             parts[p, :, at * cols : (at + 1) * cols] = part
 
     def gram(v):
         for at in range(rows):
             field = x_ref[v, :, (at + 2) * cols : (at + 3) * cols].astype(jnp.float32)
-            store_parts(at, field * weight_ref[at : at + 1, :])
-        accumulate(v, 0)
+            store_parts(at, field * weight_ref[at : at + 1, :], 3)
+        accumulate(v, 0, 3)
 
     def cross(v):
         @pl.when(me < n - 1)
@@ -175,8 +175,8 @@
             spread = dot32(near[2], band, NN)
             spread += 16.0 * (wide[1] + wide[2]) - (wide[0] + wide[3])
             scale = weight_ref[at : at + 1, :] * diff_ref[v, at : at + 1, :]
-            store_parts(at, spread * (scale / 12.0))
-        accumulate(v, 1)
+            store_parts(at, spread * (scale / 12.0), 2)
+        accumulate(v, 1, 2)
         out_copy(v).start()
 
     @pl.loop(0, variables)

time: 150 us -> 150 us (level)
  no operation moved by 1% of the time
where the time goes in v4:
time: 150 us; the launch traced here: 149 us
  Pallas kernels  149 us (99%)
    pallas_call x1, Pallas kernels, gather(): pl.pallas_call(functools.partial(gather_kernel, n, float(cells)), out_sha...  133 us
    pallas_call x1, Pallas kernels, modes(): pl.pallas_call(functools.partial(modes_kernel, float(cells)), out_shape=(...  15.9 us

profile of v4, /device:TPU:0, one launch (start us, length us, event | category | flops | bytes accessed | tf_op | source)
XLA Modules:
  0.0 149.3 jit_solution(8648117128515489702)
XLA Ops:
  0.6 132.8 %gather.1 = (bf16[4,256,2560]{2,1,0:T(8,128)(2,1)}, f32[2,2,256,128]{3,2,1,0:T(8,128)}, f32[256,256]{1,0:T(8,128)}) custom-call(bf16[16,4,256,128]{3,2,1,0:T(8,128)(2,1)} %snap_ref.1, f32[16,128]{1,0:T(8,128)} %weight_ref.1, f32[4,16,128]{2,1,0:T(8,128)} %diff_ref.3), custom_call_target="tpu_custom_call" | custom-call | tf_op jit(solution)/shard_map/gather/pallas_call | solution.py:350
  133.4 15.9 %modes.1 = (bf16[256,4,16,128]{3,2,1,0:T(8,128)(2,1)}, f32[256,256]{1,0:T(8,128)}) custom-call(f32[256,256]{1,0:T(8,128)} %get-tuple-element.5.rotation_ref, f32[2,2,256,128]{3,2,1,0:T(8,128)} %get-tuple-element.6.sums_ref, f32[4,16,128]{2,1,0:T(8,128)} %diff_ref.3, bf16[4,256,2560]{2,1,0:T(8,128)(2,1)} %get-tuple-element.7.x_ref), custom_call_target="tpu_custom_call" | custom-call | tf_op jit(solution)/shard_map/modes/pallas_call | solution.py:435
